TPU v7x, 32 devices: a whole 2x2x4 slice. The times are simulated.
32 devices in a mesh: groups: 2 (over x), seq: 16 (over z, y, core).
Axes of the slice: x: 2, y: 2, z: 4, core: 2. Of those that a mesh axis runs over, the one named last changes fastest.
Arguments:
- sequence: bfloat16 [8192, 1536], P(('groups', 'seq')), parts along dimension 0, may hold values from -6 to 6
- gain_conv: float32 [1536], replicated, may hold values from 0.25 to 1.75
- conv_weight: float32 [5, 1536], replicated, may hold values from -3 to 3
- gain_attn: float32 [1536], replicated, may hold values from 0.25 to 1.75
- w_query: bfloat16 [1536, 1024], replicated
- w_key: bfloat16 [1536, 128], replicated
- w_value: bfloat16 [1536, 192], replicated, may hold values from -0.15625 to 0.15625
- w_out: bfloat16 [1536, 1536], replicated, may hold values from -0.15625 to 0.15625
- w_left: bfloat16 [1536, 128], replicated, may hold values from -0.15625 to 0.15625
- w_right: bfloat16 [1536, 128], replicated, may hold values from -0.15625 to 0.15625
- w_pair: bfloat16 [3, 3, 128, 128], replicated, may hold values from -0.1875 to 0.1875
Outputs:
- track: bfloat16 [8192, 1536], P(('groups', 'seq')), parts along dimension 0
- pair_map: bfloat16 [512, 256, 128], P(('groups', 'seq')), parts along dimension 0
There are 2 independent parts, one for each index of `groups`. A program takes and returns all parts, laid end to end along the dimension named above; an argument that names none is the same for every part. Nothing has to cross between parts.
All inputs are finite; a program needn't handle non-finite values.
Results may differ from a plain program's by a relative error of at most 0.019.
Values may be sent and summed in bfloat16 or wider, within the bound.
A program may use at most 128 MiB of HBM per device.

v0:
```python
import jax
import jax.numpy as jnp
from jax import lax
from jax.sharding import PartitionSpec as P

HEADS = 8
POOL = 16


def extended_2(cells, sides, width):
    for axis, dim in sides:
        count = lax.axis_size(axis)
        ends = count - 1
        head = lax.slice_in_dim(cells, 0, width, axis=dim)
        tail = lax.slice_in_dim(cells, cells.shape[dim] - width, cells.shape[dim], axis=dim)
        cells = jnp.concatenate(
            [
                lax.ppermute(tail, axis, [(i, (i + 1) % count) for i in range(ends)]),
                cells,
                lax.ppermute(head, axis, [((i + 1) % count, i) for i in range(ends)]),
            ],
            axis=dim,
        )
    return cells


def rms_norm(values, gain):
    values = values.astype(jnp.float32)
    scale = lax.rsqrt(jnp.mean(values * values, axis=-1, keepdims=True) + 1e-06)
    return values * scale * gain


def attend_block(carry, queries, keys_part, values_part):
    running, totals, numer = carry
    scale = 1.0 / jnp.sqrt(jnp.float32(queries.shape[2]))
    scores = (
        jnp.einsum("qhd,kd->hqk", queries, keys_part, preferred_element_type=jnp.float32) * scale
    )
    newtop = jnp.maximum(running, jnp.max(scores, axis=-1))
    expo = jnp.exp(scores - newtop[..., None])
    factor = jnp.exp(running - newtop)
    totals = totals * factor + jnp.sum(expo, axis=-1)
    numer = numer * factor[..., None] + jnp.einsum(
        "hqk,kv->hqv", expo.astype(jnp.bfloat16), values_part, preferred_element_type=jnp.float32
    )
    return (newtop, totals, numer)


def attend_piece(carry, queries, keys_part, values_part):
    length = keys_part.shape[0]
    key_blocks = keys_part.reshape(length // 512, 512, keys_part.shape[1])
    value_blocks = values_part.reshape(length // 512, 512, values_part.shape[1])

    def stepper(state, blocks):
        return (attend_block(state, queries, blocks[0], blocks[1]), None)

    carry, unused = lax.scan(stepper, carry, (key_blocks, value_blocks))
    return carry


def local(
    sequence,
    gain_conv,
    conv_weight,
    gain_attn,
    w_query,
    w_key,
    w_value,
    w_out,
    w_left,
    w_right,
    w_pair,
):
    rows = sequence.shape[0]
    width = sequence.shape[1]
    heads = HEADS
    key_size = w_key.shape[1]
    value_size = w_value.shape[1]
    normed = rms_norm(sequence, gain_conv).astype(jnp.bfloat16)
    padded = extended_2(normed, (("seq", 0),), 2)
    convolved = jnp.zeros((rows, width), jnp.float32)
    for offset in range(conv_weight.shape[0]):
        convolved = convolved + conv_weight[offset][None, :] * padded[
            offset : offset + rows
        ].astype(jnp.float32)
    first = (sequence.astype(jnp.float32) + convolved).astype(jnp.bfloat16)
    attn_in = rms_norm(first, gain_attn).astype(jnp.bfloat16)
    queries = (
        jnp.dot(attn_in, w_query, preferred_element_type=jnp.float32)
        .astype(jnp.bfloat16)
        .reshape(rows, heads, key_size)
    )
    initial = (
        jnp.full((heads, rows), -1e30, jnp.float32),
        jnp.zeros((heads, rows), jnp.float32),
        jnp.zeros((heads, rows, value_size), jnp.float32),
    )
    keys_local = jnp.dot(attn_in, w_key, preferred_element_type=jnp.float32).astype(jnp.bfloat16)
    values_local = jnp.dot(attn_in, w_value, preferred_element_type=jnp.float32).astype(
        jnp.bfloat16
    )
    running, totals, numer = attend_piece(
        initial,
        queries,
        lax.all_gather(keys_local, "seq", axis=0, tiled=True),
        lax.all_gather(values_local, "seq", axis=0, tiled=True),
    )
    result = numer / totals[..., None]
    attended = (
        jnp.transpose(result, (1, 0, 2)).reshape(rows, heads * value_size).astype(jnp.bfloat16)
    )
    track = (
        first.astype(jnp.float32) + jnp.dot(attended, w_out, preferred_element_type=jnp.float32)
    ).astype(jnp.bfloat16)
    pooled = jnp.mean(track.astype(jnp.float32).reshape(rows // POOL, POOL, width), axis=1).astype(
        jnp.bfloat16
    )
    left = jnp.dot(pooled, w_left, preferred_element_type=jnp.float32).astype(jnp.bfloat16)
    right = jnp.dot(pooled, w_right, preferred_element_type=jnp.float32).astype(jnp.bfloat16)
    band = left.shape[0]
    right_all = lax.all_gather(right, "seq", axis=0, tiled=True)
    pair0 = (
        left.astype(jnp.float32)[:, None, :] * right_all.astype(jnp.float32)[None, :, :]
    ).astype(jnp.bfloat16)
    activated = jax.nn.gelu(pair0.astype(jnp.float32)).astype(jnp.bfloat16)
    extended = extended_2(activated, (("seq", 0),), 1)
    columns = right_all.shape[0]
    channels = right_all.shape[1]
    grid = jnp.pad(extended, ((0, 0), (1, 1), (0, 0)))
    summed = jnp.zeros((band * columns, channels), jnp.float32)
    for row_off in range(3):
        for col_off in range(3):
            window = grid[row_off : row_off + band, col_off : col_off + columns].reshape(
                band * columns, channels
            )
            summed = summed + jnp.dot(
                window, w_pair[row_off, col_off], preferred_element_type=jnp.float32
            )
    pair_map = (pair0.astype(jnp.float32) + summed.reshape(band, columns, channels)).astype(
        jnp.bfloat16
    )
    return (track, pair_map)


def solution(mesh):
    placed = (P(("groups", "seq"), None), P(), P(), P(), P(), P(), P(), P(), P(), P(), P())
    return jax.shard_map(
        local,
        mesh=mesh,
        in_specs=placed,
        out_specs=(P(("groups", "seq"), None), P(("groups", "seq"), None, None)),
        check_vma=False,
    )
```

profile of v0, /device:TPU:1, one launch (start us, length us, event | category | flops | bytes accessed | tf_op | source)
XLA Modules:
  0.0 204.6 jit_solution(1153907717193346455)
XLA Ops:
  7.2 1.5 fusion.29
  8.8 1.4 fusion.31
  10.3 4.5 %collective-permute-start = (bf16[2,1536]{1,0:T(2,128)(2,1)S(1)}, bf16[2,1536]{1,0:T(2,128)(2,1)S(1)}, u32[]{:S(2)}, u32[]{:S(2)}) collective-permute-start(bf16[2,1536]{1,0:T(2,128)(2,1)S(1)} %get-tuple-element.108), channel_id=1, source_target_pairs={{0,1},{1,2},{2,3},{3,4},{4,5},{5,6},{6,7},{7,8},{8,9},{9,10},{10,1... | collective-permute-start | bytes 18440 | tf_op jit(solution)/shard_map/ppermute | solution.py:18
  14.8 1.9 collective-permute-start.1
  16.8 2.9 %collective-permute-done.1 = bf16[2,1536]{1,0:T(2,128)(2,1)S(1)} collective-permute-done((bf16[2,1536]{1,0:T(2,128)(2,1)S(1)}, bf16[2,1536]{1,0:T(2,128)(2,1)S(1)}, u32[]{:S(2)}, u32[]{:S(2)}) %collective-permute-start.1) | collective-permute-done | bytes 6176 | tf_op jit(solution)/shard_map/ppermute | solution.py:20
  19.7 1.6 fusion.33
  21.3 0.9 copy-done.4
  22.2 1.1 convolution_convert_fusion.1
  23.4 2.3 %convolution_convert_fusion.2 = bf16[256,128]{1,0:T(8,128)(2,1)} fusion(bf16[1536,128]{1,0:T(8,128)(2,1)} %param.18, bf16[256,1536]{1,0:T(8,128)(2,1)} %copy-done.4, f32[1536]{0:T(1024)S(1)} %copy-done.11, f32[256]{0:T(256)S(1)} %add_rsqrt_fusion), kind=kOutput, calls=%fused_computation.71 | convolution fusion | flops 102268928 | bytes 1252352 | tf_op jit(solution)/shard_map/dot_general | solution.py:98
  25.7 2.2 %fusion.39 = bf16[32,8,8,128]{3,2,1,0:T(8,128)(2,1)S(1)} fusion(bf16[1536,1024]{1,0:T(8,128)(2,1)S(1)} %copy-done, bf16[256,1536]{1,0:T(8,128)(2,1)} %copy-done.4, f32[1536]{0:T(1024)S(1)} %copy-done.11, f32[256]{0:T(256)S(1)} %add_rsqrt_fusion), kind=kOutput, calls=%fused_computation.67 | convolution fusion | flops 807141376 | bytes 4463616 | tf_op jit(solution)/shard_map/dot_general | solution.py:89
  27.9 0.9 copy.22
  28.8 34.5 %all-gather.5.cloned.1.call-done = bf16[4096,192]{0,1:T(8,128)(2,1)} async-done(((bf16[256,192]{0,1:T(8,128)(2,1)}), bf16[4096,192]{0,1:T(8,128)(2,1)}) %all-gather.5.cloned.1.call-update) | async-done | bytes 1572880 | tf_op jit(solution)/shard_map/all_gather | solution.py:106
  63.3 2.7 %copy.21 = bf16[24,8,8,512]{3,2,0,1:T(8,128)(2,1)} copy(bf16[24,8,8,512]{3,2,1,0:T(8,128)(2,1)} %bitcast.116) | data formatting | bytes 3145728 | tf_op jit(solution)/shard_map/reshape | solution.py:52
  66.0 36.7 %all-gather.3.cloned.1.call-done = bf16[4096,128]{1,0:T(8,128)(2,1)} async-done(((bf16[256,128]{1,0:T(8,128)(2,1)}), bf16[4096,128]{1,0:T(8,128)(2,1)}) %all-gather.3.cloned.1.call-update) | async-done | bytes 1048592 | tf_op jit(solution)/shard_map/all_gather | solution.py:105
  102.7 53.1 %while.15 = (s32[]{:T(128)}, f32[8,256]{1,0:T(8,128)S(1)}, f32[8,256]{1,0:T(8,128)S(1)}, f32[8,256,192]{1,2,0:T(8,128)}, bf16[8,512,128]{2,1,0:T(8,128)(2,1)}, /...) while((s32[]{:T(128)}, f32[8,256]{1,0:T(8,128)S(1)}, ...), condition=%wide.region_5.6_spmd.clone, body=%wide.region_2.5_spmd.clone.sunk | while | flops 680667136 | bytes 29294768 | solution.py:57
  102.7 1.8 bitcast_reduce_fusion.2
  104.6 0.7 fusion.100
  105.3 0.7 copy-done.1
  106.0 2.2 %fusion.102 = f32[8,256,192]{1,2,0:T(8,128)S(1)} fusion(f32[8,256,192]{1,2,0:T(8,128)S(1)} %copy-done.1, f32[512,256,8]{1,0,2:T(8,128)S(1)} %get-tuple-element.160, f32[8,256]{1,0:T(8,128)S(1)} %select_maximum_fusion.2, f32[8,256]{1,0:T(8,128)S(1)} %get-tuple-element.162, pred[]{:T(512)S(6)} %compare.44, ...), kind=kOutput, calls=%fused_computation.9.clone.1 | convolution fusion | flops 406978560 | bytes 7553029 | tf_op jit(solution)/shard_map/while/body/eval_jaxpr/hqk,kv->hqv/dot_general | solution.py:43
  108.2 1.1 copy-done.2
  109.4 1.8 bitcast_reduce_fusion.2
  111.2 0.7 fusion.100
  111.9 0.7 copy-done.1
  112.6 2.2 %fusion.102 = f32[8,256,192]{1,2,0:T(8,128)S(1)} fusion(f32[8,256,192]{1,2,0:T(8,128)S(1)} %copy-done.1, f32[512,256,8]{1,0,2:T(8,128)S(1)} %get-tuple-element.160, f32[8,256]{1,0:T(8,128)S(1)} %select_maximum_fusion.2, f32[8,256]{1,0:T(8,128)S(1)} %get-tuple-element.162, pred[]{:T(512)S(6)} %compare.44, ...), kind=kOutput, calls=%fused_computation.9.clone.1 | convolution fusion | flops 406978560 | bytes 7553029 | tf_op jit(solution)/shard_map/while/body/eval_jaxpr/hqk,kv->hqv/dot_general | solution.py:43
  114.9 1.1 copy-done.2
  116.0 1.8 bitcast_reduce_fusion.2
  117.9 0.7 fusion.100
  118.6 0.7 copy-done.1
  119.3 2.2 %fusion.102 = f32[8,256,192]{1,2,0:T(8,128)S(1)} fusion(f32[8,256,192]{1,2,0:T(8,128)S(1)} %copy-done.1, f32[512,256,8]{1,0,2:T(8,128)S(1)} %get-tuple-element.160, f32[8,256]{1,0:T(8,128)S(1)} %select_maximum_fusion.2, f32[8,256]{1,0:T(8,128)S(1)} %get-tuple-element.162, pred[]{:T(512)S(6)} %compare.44, ...), kind=kOutput, calls=%fused_computation.9.clone.1 | convolution fusion | flops 406978560 | bytes 7553029 | tf_op jit(solution)/shard_map/while/body/eval_jaxpr/hqk,kv->hqv/dot_general | solution.py:43
  121.5 1.1 copy-done.2
  122.6 1.8 bitcast_reduce_fusion.2
  124.5 0.7 fusion.100
  125.2 0.7 copy-done.1
  125.9 2.2 %fusion.102 = f32[8,256,192]{1,2,0:T(8,128)S(1)} fusion(f32[8,256,192]{1,2,0:T(8,128)S(1)} %copy-done.1, f32[512,256,8]{1,0,2:T(8,128)S(1)} %get-tuple-element.160, f32[8,256]{1,0:T(8,128)S(1)} %select_maximum_fusion.2, f32[8,256]{1,0:T(8,128)S(1)} %get-tuple-element.162, pred[]{:T(512)S(6)} %compare.44, ...), kind=kOutput, calls=%fused_computation.9.clone.1 | convolution fusion | flops 406978560 | bytes 7553029 | tf_op jit(solution)/shard_map/while/body/eval_jaxpr/hqk,kv->hqv/dot_general | solution.py:43
  128.1 1.1 copy-done.2
  129.3 1.8 bitcast_reduce_fusion.2
  131.1 0.7 fusion.100
  131.9 0.7 copy-done.1
  132.5 2.2 %fusion.102 = f32[8,256,192]{1,2,0:T(8,128)S(1)} fusion(f32[8,256,192]{1,2,0:T(8,128)S(1)} %copy-done.1, f32[512,256,8]{1,0,2:T(8,128)S(1)} %get-tuple-element.160, f32[8,256]{1,0:T(8,128)S(1)} %select_maximum_fusion.2, f32[8,256]{1,0:T(8,128)S(1)} %get-tuple-element.162, pred[]{:T(512)S(6)} %compare.44, ...), kind=kOutput, calls=%fused_computation.9.clone.1 | convolution fusion | flops 406978560 | bytes 7553029 | tf_op jit(solution)/shard_map/while/body/eval_jaxpr/hqk,kv->hqv/dot_general | solution.py:43
  134.8 1.1 copy-done.2
  135.9 1.8 bitcast_reduce_fusion.2
  137.8 0.7 fusion.100
  138.5 0.7 copy-done.1
  139.2 2.2 %fusion.102 = f32[8,256,192]{1,2,0:T(8,128)S(1)} fusion(f32[8,256,192]{1,2,0:T(8,128)S(1)} %copy-done.1, f32[512,256,8]{1,0,2:T(8,128)S(1)} %get-tuple-element.160, f32[8,256]{1,0:T(8,128)S(1)} %select_maximum_fusion.2, f32[8,256]{1,0:T(8,128)S(1)} %get-tuple-element.162, pred[]{:T(512)S(6)} %compare.44, ...), kind=kOutput, calls=%fused_computation.9.clone.1 | convolution fusion | flops 406978560 | bytes 7553029 | tf_op jit(solution)/shard_map/while/body/eval_jaxpr/hqk,kv->hqv/dot_general | solution.py:43
  141.4 1.1 copy-done.2
  142.5 1.8 bitcast_reduce_fusion.2
  144.4 0.7 fusion.100
  145.1 0.7 copy-done.1
  145.8 2.2 %fusion.102 = f32[8,256,192]{1,2,0:T(8,128)S(1)} fusion(f32[8,256,192]{1,2,0:T(8,128)S(1)} %copy-done.1, f32[512,256,8]{1,0,2:T(8,128)S(1)} %get-tuple-element.160, f32[8,256]{1,0:T(8,128)S(1)} %select_maximum_fusion.2, f32[8,256]{1,0:T(8,128)S(1)} %get-tuple-element.162, pred[]{:T(512)S(6)} %compare.44, ...), kind=kOutput, calls=%fused_computation.9.clone.1 | convolution fusion | flops 406978560 | bytes 7553029 | tf_op jit(solution)/shard_map/while/body/eval_jaxpr/hqk,kv->hqv/dot_general | solution.py:43
  148.0 1.1 copy-done.2
  149.2 1.8 bitcast_reduce_fusion.2
  151.0 0.7 fusion.100
  151.8 0.7 copy-done.1
  152.4 2.2 %fusion.102 = f32[8,256,192]{1,2,0:T(8,128)S(1)} fusion(f32[8,256,192]{1,2,0:T(8,128)S(1)} %copy-done.1, f32[512,256,8]{1,0,2:T(8,128)S(1)} %get-tuple-element.160, f32[8,256]{1,0:T(8,128)S(1)} %select_maximum_fusion.2, f32[8,256]{1,0:T(8,128)S(1)} %get-tuple-element.162, pred[]{:T(512)S(6)} %compare.44, ...), kind=kOutput, calls=%fused_computation.9.clone.1 | convolution fusion | flops 406978560 | bytes 7553029 | tf_op jit(solution)/shard_map/while/body/eval_jaxpr/hqk,kv->hqv/dot_general | solution.py:43
  154.7 1.1 copy-done.2
  155.8 1.6 divide_convert_fusion
  157.5 4.8 %convert_reduce_fusion = (f32[16,1536]{1,0:T(8,128)S(1)}, bf16[256,1536]{1,0:T(8,128)(2,1)}) fusion(bf16[256,1536]{0,1:T(8,128)(2,1)S(1)} %bitcast.117, bf16[1536,1536]{1,0:T(8,128)(2,1)} %param.20, bf16[256,1536]{1,0:T(8,128)(2,1)S(1)} %copy-done.5), kind=kOutput, calls=%fused_computation.61 | convolution fusion | flops 1209901056 | bytes 7176192 | tf_op jit(solution)/shard_map/dot_general | solution.py:113
  162.6 19.7 %all_gather.11 = bf16[256,128]{1,0:T(8,128)(2,1)S(1)} all-gather(bf16[16,128]{1,0:T(8,128)(2,1)S(1)} %convolution_convert_fusion.3), channel_id=1, replica_groups=mesh['groups'=2,'seq'=16] {'seq'}, dimensions={0}, use_global_device_ids=true | all-gather | bytes 69632 | tf_op jit(solution)/shard_map/all_gather | solution.py:121
  182.3 0.8 fusion.27
  183.1 1.9 collective-permute-start.2
  185.0 2.6 %collective-permute-start.3 = (bf16[1,256,128]{2,1,0:T(8,128)(2,1)S(1)}, bf16[1,256,128]{2,1,0:T(8,128)(2,1)S(1)}, u32[]{:S(2)}, u32[]{:S(2)}) collective-permute-start(bf16[1,256,128]{2,1,0:T(8,128)(2,1)S(1)} %get-tuple-element.107), channel_id=1, source_target_pairs={{1,0},{2,1},{3,2},{4,3},{5,4},{6,5},{7,6},{8,7},{9,8},{10,9},{11,1... | collective-permute-start | bytes 196616 | tf_op jit(solution)/shard_map/ppermute | solution.py:20
  187.6 3.0 %collective-permute-done.3 = bf16[1,256,128]{2,1,0:T(8,128)(2,1)S(1)} collective-permute-done((bf16[1,256,128]{2,1,0:T(8,128)(2,1)S(1)}, bf16[1,256,128]{2,1,0:T(8,128)(2,1)S(1)}, u32[]{:S(2)}, u32[]{:S(2)}) %collective-permute-start.3) | collective-permute-done | bytes 65568 | tf_op jit(solution)/shard_map/ppermute | solution.py:20
  191.0 1.5 fusion.71
  196.5 1.3 fusion.28
  (87 shorter events, 5.1 us)
Async XLA Ops:
  7.2 18.6 %copy-start = (bf16[1536,1024]{1,0:T(8,128)(2,1)S(1)}, bf16[1536,1024]{1,0:T(8,128)(2,1)}, u32[]{:S(2)}) copy-start(bf16[1536,1024]{1,0:T(8,128)(2,1)} %param.17) | copy-start | bytes 9437188
  7.2 9.5 %copy-start.9 = (f32[5,1536]{1,0:T(8,128)S(1)}, f32[5,1536]{1,0:T(8,128)}, u32[]{:S(2)}) copy-start(f32[5,1536]{1,0:T(8,128)} %param.15) | copy-start | bytes 92164
  7.2 56.1 %all-gather.5.cloned.1.call-start = ((), (), s32[]{:S(2)}) async-start(), calls=%async_computation.1 | async-start | bytes 1671168 | tf_op jit(solution)/shard_map/all_gather | solution.py:106
  7.2 12.5 %copy-start.3 = (bf16[256,1536]{1,0:T(8,128)(2,1)S(1)}, bf16[256,1536]{1,0:T(8,128)(2,1)}, u32[]{:S(2)}) copy-start(bf16[256,1536]{1,0:T(8,128)(2,1)} %param.13) | copy-start | bytes 2359300
  8.8 13.4 %copy-start.10 = (bf16[1536,192]{0,1:T(8,128)(2,1)S(1)}, bf16[1536,192]{0,1:T(8,128)(2,1)}, u32[]{:S(2)}) copy-start(bf16[1536,192]{0,1:T(8,128)(2,1)} %param.19) | copy-start | bytes 1769476
  8.8 13.4 %copy-start.11 = (f32[1536]{0:T(1024)S(1)}, f32[1536]{0:T(1024)}, u32[]{:S(2)}) copy-start(f32[1536]{0:T(1024)} %param.16) | copy-start | bytes 18436
  10.3 6.6 %collective-permute-start = (bf16[2,1536]{1,0:T(2,128)(2,1)S(1)}, bf16[2,1536]{1,0:T(2,128)(2,1)S(1)}, u32[]{:S(2)}, u32[]{:S(2)}) collective-permute-start(bf16[2,1536]{1,0:T(2,128)(2,1)S(1)} %get-tuple-element.108), channel_id=1, source_target_pairs={{0,1},{1,2},{2,3},{3,4},{4,5},{5,6},{6,7},{7,8},{8,9},{9,10},{10,1... | collective-permute-start | bytes 18440 | tf_op jit(solution)/shard_map/ppermute | solution.py:18
  14.8 4.9 %collective-permute-start.1 = (bf16[2,1536]{1,0:T(2,128)(2,1)S(1)}, bf16[2,1536]{1,0:T(2,128)(2,1)S(1)}, u32[]{:S(2)}, u32[]{:S(2)}) collective-permute-start(bf16[2,1536]{1,0:T(2,128)(2,1)S(1)} %get-tuple-element.109), channel_id=1, source_target_pairs={{1,0},{2,1},{3,2},{4,3},{5,4},{6,5},{7,6},{8,7},{9,8},{10,9},{11,1... | collective-permute-start | bytes 18440 | tf_op jit(solution)/shard_map/ppermute | solution.py:20
  21.3 0.9 copy-start.4
  23.3 79.4 %all-gather.3.cloned.1.call-start = ((), (), s32[]{:S(2)}) async-start(), calls=%async_computation | async-start | bytes 1114112 | tf_op jit(solution)/shard_map/all_gather | solution.py:105
  104.6 1.4 copy-start.1
  108.2 1.2 copy-start.2
  111.2 1.4 copy-start.1
  114.8 1.2 copy-start.2
  117.9 1.4 copy-start.1
  121.5 1.2 copy-start.2
  124.5 1.4 copy-start.1
  128.1 1.2 copy-start.2
  131.1 1.4 copy-start.1
  134.8 1.2 copy-start.2
  137.8 1.4 copy-start.1
  141.4 1.2 copy-start.2
  144.4 1.4 copy-start.1
  148.0 1.2 copy-start.2
  151.0 1.4 copy-start.1
  154.7 1.2 copy-start.2
  155.8 1.6 copy-start.5
  157.4 4.9 %copy-start.7 = (bf16[1536,128]{1,0:T(8,128)(2,1)S(1)}, bf16[1536,128]{1,0:T(8,128)(2,1)}, u32[]{:S(2)}) copy-start(bf16[1536,128]{1,0:T(8,128)(2,1)} %param.22) | copy-start | bytes 1179652
  157.5 5.0 %copy-start.6 = (bf16[1536,128]{1,0:T(8,128)(2,1)S(1)}, bf16[1536,128]{1,0:T(8,128)(2,1)}, u32[]{:S(2)}) copy-start(bf16[1536,128]{1,0:T(8,128)(2,1)} %param.21) | copy-start | bytes 1179652
  183.1 4.5 %collective-permute-start.2 = (bf16[1,256,128]{2,1,0:T(8,128)(2,1)S(1)}, bf16[1,256,128]{2,1,0:T(8,128)(2,1)S(1)}, u32[]{:S(2)}, u32[]{:S(2)}) collective-permute-start(bf16[1,256,128]{2,1,0:T(8,128)(2,1)S(1)} %get-tuple-element.106), channel_id=1, source_target_pairs={{0,1},{1,2},{2,3},{3,4},{4,5},{5,6},{6,7},{7,8},{8,9},{9,10},{10,1... | collective-permute-start | bytes 196616 | tf_op jit(solution)/shard_map/ppermute | solution.py:18
  185.0 5.6 %collective-permute-start.3 = (bf16[1,256,128]{2,1,0:T(8,128)(2,1)S(1)}, bf16[1,256,128]{2,1,0:T(8,128)(2,1)S(1)}, u32[]{:S(2)}, u32[]{:S(2)}) collective-permute-start(bf16[1,256,128]{2,1,0:T(8,128)(2,1)S(1)} %get-tuple-element.107), channel_id=1, source_target_pairs={{1,0},{2,1},{3,2},{4,3},{5,4},{6,5},{7,6},{8,7},{9,8},{10,9},{11,1... | collective-permute-start | bytes 196616 | tf_op jit(solution)/shard_map/ppermute | solution.py:20
  191.0 1.5 copy-start.8
Sparse Core Ops, SparseCore 0:
  23.5 39.7 all-gather.4
  65.4 37.2 all-gather.2
where the time goes:
time: 206 us; the launch traced here: 205 us
  waiting for transfers between devices  77.1 us (37%)
  matrix products  46.8 us (23%)
  local copies, waits for them, and re-layouts  20.7 us (10%)
  blocking collectives  19.7 us (10%)
  between operations  14.4 us (7%)
  other arithmetic  14.3 us (7%)
  starting transfers between devices  11 us (5%)
    all_gather x1, waiting for transfers between devices, local(): lax.all_gather(keys_local, 'seq', axis=0, tiled=True)  36.7 us
    all_gather x1, waiting for transfers between devices, local(): lax.all_gather(values_local, 'seq', axis=0, tiled=True)  34.5 us
    all_gather x1, blocking collectives, local(): right_all = lax.all_gather(right, 'seq', axis=0, tiled=True)  19.7 us
    dot_general x8, matrix products, attend_block(): jnp.einsum('hqk,kv->hqv', expo.astype(jnp.bfloat16), values_part, preferr...  17.7 us
    dot_general x8, matrix products, attend_block(): jnp.einsum('qhd,kd->hqk', queries, keys_part, preferred_element_type=jnp....  14.6 us
    while x40, local copies, waits for them, and re-layouts  14.6 us
    ppermute x2, starting transfers between devices, extended_2(): lax.ppermute(tail, axis, [(i, (i + 1) % count) for i in range(ends)])  6.45 us
    ppermute x2, waiting for transfers between devices, extended_2(): lax.ppermute(head, axis, [((i + 1) % count, i) for i in range(ends)])  5.89 us
  transfers between devices with their start and end apart: 6, of which 4 were waited for; matrix products, arithmetic and copies ran while one was open for 4% of the time, Pallas kernels for 0%

commit v1 on v0

--- a/solution.py
+++ b/solution.py
@@ -5,6 +5,28 @@
 
 HEADS = 8
 POOL = 16
+
+
+def laid_out(blocks, dim):
+    blocks = jnp.moveaxis(blocks, 0, dim)
+    lengths = blocks.shape
+    return blocks.reshape(*lengths[:dim], lengths[dim] * lengths[dim + 1], *lengths[dim + 2 :])
+
+
+def collected_by_bits(array, axis):
+    devices = lax.axis_size(axis)
+    tiles = array[None]
+    for level in range(devices.bit_length() - 1):
+        bit = 1 << level
+        received = lax.ppermute(tiles, axis, [(i, i ^ bit) for i in range(devices)])
+        both = jnp.stack([tiles, received])
+        upper = lax.axis_index(axis) >> level & 1
+        tiles = jnp.where(upper == 0, both, both[::-1]).reshape(-1, *array.shape)
+    return tiles
+
+
+def collect(x, axis, dim):
+    return laid_out(collected_by_bits(x, axis), dim)
 
 
 def extended_2(cells, sides, width):
@@ -102,7 +124,7 @@
     running, totals, numer = attend_piece(
         initial,
         queries,
-        lax.all_gather(keys_local, "seq", axis=0, tiled=True),
+        collect(keys_local, "seq", 0),
         lax.all_gather(values_local, "seq", axis=0, tiled=True),
     )
     result = numer / totals[..., None]

time: 206 us -> 187 us (0.908)
  waiting for transfers between devices: 77.1 us -> 45.9 us
  starting transfers between devices: 11 us -> 17.4 us
  other arithmetic: 14.3 us -> 18.9 us
  blocking collectives: 19.7 us -> 22.1 us
    ppermute x0 -> x4, waiting for transfers between devices: none -> 40 us  [collected_by_bits(): received = lax.ppermute(tiles, axis, [(i, i ^ bit) for i in range(devices)])]
    all_gather x1 -> x0, waiting for transfers between devices: 36.7 us -> none  [local(): lax.all_gather(keys_local, 'seq', axis=0, tiled=True)]
    all_gather x1, waiting for transfers between devices: 34.5 us -> 0.01 us  [local(): lax.all_gather(values_local, 'seq', axis=0, tiled=True)]
    ppermute x0 -> x4, starting transfers between devices: none -> 6.4 us  [collected_by_bits(): received = lax.ppermute(tiles, axis, [(i, i ^ bit) for i in range(devices)])]
    all_gather x1, blocking collectives: 19.7 us -> 22.1 us  [local(): right_all = lax.all_gather(right, 'seq', axis=0, tiled=True)]
    another operation x0 -> x5, other arithmetic: none -> 2.38 us  [collected_by_bits(): both = jnp.stack([tiles, received])]
    select_n x0 -> x3, other arithmetic: none -> 2.16 us  [collected_by_bits(): tiles = jnp.where(upper == 0, both, both[::-1]).reshape(-1, *array.shape)]
  transfers between devices with their start and end apart: 6 -> 9, of which waited for: 4 -> 6; matrix products, arithmetic and copies ran while one was open for 4% -> 5% of each run, Pallas kernels for 0% -> 0%
where the time goes in v1:
time: 187 us; the launch traced here: 186 us
  matrix products  46.2 us (25%)
  waiting for transfers between devices  45.9 us (25%)
  blocking collectives  22.1 us (12%)
  local copies, waits for them, and re-layouts  20.6 us (11%)
  other arithmetic  18.9 us (10%)
  starting transfers between devices  17.4 us (9%)
  between operations  14.4 us (8%)
    ppermute x4, waiting for transfers between devices, collected_by_bits(): received = lax.ppermute(tiles, axis, [(i, i ^ bit) for i in range(devices)])  40 us
    all_gather x1, blocking collectives, local(): right_all = lax.all_gather(right, 'seq', axis=0, tiled=True)  22.1 us
    dot_general x8, matrix products, attend_block(): jnp.einsum('hqk,kv->hqv', expo.astype(jnp.bfloat16), values_part, preferr...  17.6 us
    dot_general x8, matrix products, attend_block(): jnp.einsum('qhd,kd->hqk', queries, keys_part, preferred_element_type=jnp....  14.6 us
    while x40, local copies, waits for them, and re-layouts  14.5 us
    ppermute x2, starting transfers between devices, extended_2(): lax.ppermute(tail, axis, [(i, (i + 1) % count) for i in range(ends)])  6.45 us
    ppermute x4, starting transfers between devices, collected_by_bits(): received = lax.ppermute(tiles, axis, [(i, i ^ bit) for i in range(devices)])  6.4 us
    ppermute x2, waiting for transfers between devices, extended_2(): lax.ppermute(head, axis, [((i + 1) % count, i) for i in range(ends)])  5.89 us
  transfers between devices with their start and end apart: 9, of which 6 were waited for; matrix products, arithmetic and copies ran while one was open for 5% of the time, Pallas kernels for 0%

profile of v1, /device:TPU:1, one launch (start us, length us, event | category | flops | bytes accessed | tf_op | source)
XLA Modules:
  0.0 186.0 jit_solution(13273620033550761987)
XLA Ops:
  7.2 1.5 fusion.29
  8.8 1.4 fusion.31
  10.3 4.5 %collective-permute-start = (bf16[2,1536]{1,0:T(2,128)(2,1)S(1)}, bf16[2,1536]{1,0:T(2,128)(2,1)S(1)}, u32[]{:S(2)}, u32[]{:S(2)}) collective-permute-start(bf16[2,1536]{1,0:T(2,128)(2,1)S(1)} %get-tuple-element.108), channel_id=1, source_target_pairs={{0,1},{1,2},{2,3},{3,4},{4,5},{5,6},{6,7},{7,8},{8,9},{9,10},{10,1... | collective-permute-start | bytes 18440 | tf_op jit(solution)/shard_map/ppermute | solution.py:40
  14.8 1.9 %collective-permute-start.1 = (bf16[2,1536]{1,0:T(2,128)(2,1)S(1)}, bf16[2,1536]{1,0:T(2,128)(2,1)S(1)}, u32[]{:S(2)}, u32[]{:S(2)}) collective-permute-start(bf16[2,1536]{1,0:T(2,128)(2,1)S(1)} %get-tuple-element.109), channel_id=1, source_target_pairs={{1,0},{2,1},{3,2},{4,3},{5,4},{6,5},{7,6},{8,7},{9,8},{10,9},{11,1... | collective-permute-start | bytes 18440 | tf_op jit(solution)/shard_map/ppermute | solution.py:42
  16.8 2.9 %collective-permute-done.1 = bf16[2,1536]{1,0:T(2,128)(2,1)S(1)} collective-permute-done((bf16[2,1536]{1,0:T(2,128)(2,1)S(1)}, bf16[2,1536]{1,0:T(2,128)(2,1)S(1)}, u32[]{:S(2)}, u32[]{:S(2)}) %collective-permute-start.1) | collective-permute-done | bytes 6176 | tf_op jit(solution)/shard_map/ppermute | solution.py:42
  19.7 1.6 fusion.33
  21.3 0.9 copy-done.4
  22.2 1.1 convolution_convert_fusion.1
  23.4 1.7 convolution_convert_fusion.2
  25.1 1.2 collective-permute-done.2
  26.4 2.2 %collective-permute-start.3 = (bf16[2,256,128]{2,1,0:T(8,128)(2,1)S(1)}, bf16[2,256,128]{2,1,0:T(8,128)(2,1)S(1)}, u32[]{:S(2)}, u32[]{:S(2)}) collective-permute-start(bf16[2,256,128]{2,1,0:T(8,128)(2,1)S(1)} %get-tuple-element.111), channel_id=1, source_target_pairs={{0,2},{1,3},{2,0},{3,1},{4,6},{5,7},{6,4},{7,5},{8,10},{9,11},{10,... | collective-permute-start | bytes 393224 | tf_op jit(solution)/shard_map/ppermute | solution.py:21
  28.6 3.7 %collective-permute-done.3 = bf16[2,256,128]{2,1,0:T(8,128)(2,1)S(1)} collective-permute-done((bf16[2,256,128]{2,1,0:T(8,128)(2,1)S(1)}, bf16[2,256,128]{2,1,0:T(8,128)(2,1)S(1)}, u32[]{:S(2)}, u32[]{:S(2)}) %collective-permute-start.3) | collective-permute-done | bytes 131104 | tf_op jit(solution)/shard_map/ppermute | solution.py:21
  32.4 1.4 collective-permute-start.4
  33.8 8.5 %collective-permute-done.4 = bf16[4,256,128]{2,1,0:T(8,128)(2,1)} collective-permute-done((bf16[4,256,128]{2,1,0:T(8,128)(2,1)S(1)}, bf16[4,256,128]{2,1,0:T(8,128)(2,1)}, u32[]{:S(2)}, u32[]{:S(2)}) %collective-permute-start.4) | collective-permute-done | bytes 262176 | tf_op jit(solution)/shard_map/ppermute | solution.py:21
  42.3 1.0 pad_maximum_fusion.5
  43.3 0.9 reverse_select_fusion.1
  44.2 2.7 %collective-permute-start.5 = (bf16[8,256,128]{2,1,0:T(8,128)(2,1)}, bf16[8,256,128]{2,1,0:T(8,128)(2,1)}, u32[]{:S(2)}, u32[]{:S(2)}) collective-permute-start(bf16[8,256,128]{2,1,0:T(8,128)(2,1)} %bitcast.10), channel_id=1, source_target_pairs={{0,8},{1,9},{2,10},{3,11},{4,12},{5,13},{6,14},{7,15},{8,0},{9,1},... | collective-permute-start | bytes 1572872 | tf_op jit(solution)/shard_map/ppermute | solution.py:21
  46.9 2.2 %fusion.39 = bf16[32,8,8,128]{3,2,1,0:T(8,128)(2,1)S(1)} fusion(bf16[1536,1024]{1,0:T(8,128)(2,1)S(1)} %copy-done, bf16[256,1536]{1,0:T(8,128)(2,1)} %copy-done.4, f32[1536]{0:T(1024)S(1)} %copy-done.11, f32[256]{0:T(256)S(1)} %add_rsqrt_fusion), kind=kOutput, calls=%fused_computation.68 | convolution fusion | flops 807141376 | bytes 4463616 | tf_op jit(solution)/shard_map/dot_general | solution.py:111
  49.1 0.9 copy.22
  50.0 26.6 %collective-permute-done.5 = bf16[8,256,128]{2,1,0:T(8,128)(2,1)} collective-permute-done((bf16[8,256,128]{2,1,0:T(8,128)(2,1)}, bf16[8,256,128]{2,1,0:T(8,128)(2,1)}, u32[]{:S(2)}, u32[]{:S(2)}) %collective-permute-start.5) | collective-permute-done | bytes 524320 | tf_op jit(solution)/shard_map/ppermute | solution.py:21
  76.6 1.3 pad_maximum_fusion.2
  77.9 1.2 reverse_select_fusion
  79.1 2.7 %copy.21 = bf16[24,8,8,512]{3,2,0,1:T(8,128)(2,1)} copy(bf16[24,8,8,512]{3,2,1,0:T(8,128)(2,1)} %bitcast.131) | data formatting | bytes 3145728 | tf_op jit(solution)/shard_map/reshape | solution.py:74
  81.8 53.0 %while.15 = (s32[]{:T(128)}, f32[8,256]{1,0:T(8,128)S(1)}, f32[8,256]{1,0:T(8,128)S(1)}, f32[8,256,192]{1,2,0:T(8,128)}, bf16[8,512,128]{2,1,0:T(8,128)(2,1)}, /...) while((s32[]{:T(128)}, f32[8,256]{1,0:T(8,128)S(1)}, ...), condition=%wide.region_5.6_spmd.clone, body=%wide.region_2.5_spmd.clone.sunk | while | flops 680667136 | bytes 29294768 | solution.py:79
  81.8 1.8 bitcast_reduce_fusion.2
  83.7 0.7 fusion.102
  85.1 2.2 %fusion.104 = f32[8,256,192]{1,2,0:T(8,128)S(1)} fusion(f32[8,256,192]{1,2,0:T(8,128)S(1)} %copy-done.1, f32[512,256,8]{1,0,2:T(8,128)S(1)} %get-tuple-element.162, f32[8,256]{1,0:T(8,128)S(1)} %select_maximum_fusion.2, f32[8,256]{1,0:T(8,128)S(1)} %get-tuple-element.164, pred[]{:T(512)S(6)} %compare.44, ...), kind=kOutput, calls=%fused_computation.9.clone.1 | convolution fusion | flops 406978560 | bytes 7553029 | tf_op jit(solution)/shard_map/while/body/eval_jaxpr/hqk,kv->hqv/dot_general | solution.py:65
  87.3 1.1 copy-done.2
  88.5 1.8 bitcast_reduce_fusion.2
  90.3 0.7 fusion.102
  91.7 2.2 %fusion.104 = f32[8,256,192]{1,2,0:T(8,128)S(1)} fusion(f32[8,256,192]{1,2,0:T(8,128)S(1)} %copy-done.1, f32[512,256,8]{1,0,2:T(8,128)S(1)} %get-tuple-element.162, f32[8,256]{1,0:T(8,128)S(1)} %select_maximum_fusion.2, f32[8,256]{1,0:T(8,128)S(1)} %get-tuple-element.164, pred[]{:T(512)S(6)} %compare.44, ...), kind=kOutput, calls=%fused_computation.9.clone.1 | convolution fusion | flops 406978560 | bytes 7553029 | tf_op jit(solution)/shard_map/while/body/eval_jaxpr/hqk,kv->hqv/dot_general | solution.py:65
  93.9 1.1 copy-done.2
  95.1 1.8 bitcast_reduce_fusion.2
  96.9 0.7 fusion.102
  98.3 2.2 %fusion.104 = f32[8,256,192]{1,2,0:T(8,128)S(1)} fusion(f32[8,256,192]{1,2,0:T(8,128)S(1)} %copy-done.1, f32[512,256,8]{1,0,2:T(8,128)S(1)} %get-tuple-element.162, f32[8,256]{1,0:T(8,128)S(1)} %select_maximum_fusion.2, f32[8,256]{1,0:T(8,128)S(1)} %get-tuple-element.164, pred[]{:T(512)S(6)} %compare.44, ...), kind=kOutput, calls=%fused_computation.9.clone.1 | convolution fusion | flops 406978560 | bytes 7553029 | tf_op jit(solution)/shard_map/while/body/eval_jaxpr/hqk,kv->hqv/dot_general | solution.py:65
  100.6 1.1 copy-done.2
  101.7 1.8 bitcast_reduce_fusion.2
  103.5 0.7 fusion.102
  104.9 2.2 %fusion.104 = f32[8,256,192]{1,2,0:T(8,128)S(1)} fusion(f32[8,256,192]{1,2,0:T(8,128)S(1)} %copy-done.1, f32[512,256,8]{1,0,2:T(8,128)S(1)} %get-tuple-element.162, f32[8,256]{1,0:T(8,128)S(1)} %select_maximum_fusion.2, f32[8,256]{1,0:T(8,128)S(1)} %get-tuple-element.164, pred[]{:T(512)S(6)} %compare.44, ...), kind=kOutput, calls=%fused_computation.9.clone.1 | convolution fusion | flops 406978560 | bytes 7553029 | tf_op jit(solution)/shard_map/while/body/eval_jaxpr/hqk,kv->hqv/dot_general | solution.py:65
  107.2 1.1 copy-done.2
  108.3 1.8 bitcast_reduce_fusion.2
  110.2 0.7 fusion.102
  111.6 2.2 %fusion.104 = f32[8,256,192]{1,2,0:T(8,128)S(1)} fusion(f32[8,256,192]{1,2,0:T(8,128)S(1)} %copy-done.1, f32[512,256,8]{1,0,2:T(8,128)S(1)} %get-tuple-element.162, f32[8,256]{1,0:T(8,128)S(1)} %select_maximum_fusion.2, f32[8,256]{1,0:T(8,128)S(1)} %get-tuple-element.164, pred[]{:T(512)S(6)} %compare.44, ...), kind=kOutput, calls=%fused_computation.9.clone.1 | convolution fusion | flops 406978560 | bytes 7553029 | tf_op jit(solution)/shard_map/while/body/eval_jaxpr/hqk,kv->hqv/dot_general | solution.py:65
  113.8 1.1 copy-done.2
  114.9 1.8 bitcast_reduce_fusion.2
  118.2 2.2 %fusion.104 = f32[8,256,192]{1,2,0:T(8,128)S(1)} fusion(f32[8,256,192]{1,2,0:T(8,128)S(1)} %copy-done.1, f32[512,256,8]{1,0,2:T(8,128)S(1)} %get-tuple-element.162, f32[8,256]{1,0:T(8,128)S(1)} %select_maximum_fusion.2, f32[8,256]{1,0:T(8,128)S(1)} %get-tuple-element.164, pred[]{:T(512)S(6)} %compare.44, ...), kind=kOutput, calls=%fused_computation.9.clone.1 | convolution fusion | flops 406978560 | bytes 7553029 | tf_op jit(solution)/shard_map/while/body/eval_jaxpr/hqk,kv->hqv/dot_general | solution.py:65
  120.4 1.1 copy-done.2
  121.5 1.8 bitcast_reduce_fusion.2
  123.4 0.7 fusion.102
  124.8 2.2 %fusion.104 = f32[8,256,192]{1,2,0:T(8,128)S(1)} fusion(f32[8,256,192]{1,2,0:T(8,128)S(1)} %copy-done.1, f32[512,256,8]{1,0,2:T(8,128)S(1)} %get-tuple-element.162, f32[8,256]{1,0:T(8,128)S(1)} %select_maximum_fusion.2, f32[8,256]{1,0:T(8,128)S(1)} %get-tuple-element.164, pred[]{:T(512)S(6)} %compare.44, ...), kind=kOutput, calls=%fused_computation.9.clone.1 | convolution fusion | flops 406978560 | bytes 7553029 | tf_op jit(solution)/shard_map/while/body/eval_jaxpr/hqk,kv->hqv/dot_general | solution.py:65
  127.0 1.1 copy-done.2
  128.2 1.8 bitcast_reduce_fusion.2
  130.0 0.7 fusion.102
  131.4 2.2 %fusion.104 = f32[8,256,192]{1,2,0:T(8,128)S(1)} fusion(f32[8,256,192]{1,2,0:T(8,128)S(1)} %copy-done.1, f32[512,256,8]{1,0,2:T(8,128)S(1)} %get-tuple-element.162, f32[8,256]{1,0:T(8,128)S(1)} %select_maximum_fusion.2, f32[8,256]{1,0:T(8,128)S(1)} %get-tuple-element.164, pred[]{:T(512)S(6)} %compare.44, ...), kind=kOutput, calls=%fused_computation.9.clone.1 | convolution fusion | flops 406978560 | bytes 7553029 | tf_op jit(solution)/shard_map/while/body/eval_jaxpr/hqk,kv->hqv/dot_general | solution.py:65
  133.7 1.1 copy-done.2
  134.8 1.6 divide_convert_fusion
  136.4 4.8 %convert_reduce_fusion = (f32[16,1536]{1,0:T(8,128)S(1)}, bf16[256,1536]{1,0:T(8,128)(2,1)}) fusion(bf16[256,1536]{0,1:T(8,128)(2,1)S(1)} %bitcast.134, bf16[1536,1536]{1,0:T(8,128)(2,1)} %param.20, bf16[256,1536]{1,0:T(8,128)(2,1)S(1)} %copy-done.5), kind=kOutput, calls=%fused_computation.61 | convolution fusion | flops 1209901056 | bytes 7176192 | tf_op jit(solution)/shard_map/dot_general | solution.py:135
  141.6 22.1 %all_gather.7 = bf16[256,128]{1,0:T(8,128)(2,1)S(1)} all-gather(bf16[16,128]{1,0:T(8,128)(2,1)S(1)} %convolution_convert_fusion.3), channel_id=1, replica_groups=mesh['groups'=2,'seq'=16] {'seq'}, dimensions={0}, use_global_device_ids=true | all-gather | bytes 69632 | tf_op jit(solution)/shard_map/all_gather | solution.py:143
  163.7 0.8 fusion.27
  164.5 1.9 %collective-permute-start.6 = (bf16[1,256,128]{2,1,0:T(8,128)(2,1)S(1)}, bf16[1,256,128]{2,1,0:T(8,128)(2,1)S(1)}, u32[]{:S(2)}, u32[]{:S(2)}) collective-permute-start(bf16[1,256,128]{2,1,0:T(8,128)(2,1)S(1)} %get-tuple-element.106), channel_id=1, source_target_pairs={{0,1},{1,2},{2,3},{3,4},{4,5},{5,6},{6,7},{7,8},{8,9},{9,10},{10,1... | collective-permute-start | bytes 196616 | tf_op jit(solution)/shard_map/ppermute | solution.py:40
  166.5 2.6 %collective-permute-start.7 = (bf16[1,256,128]{2,1,0:T(8,128)(2,1)S(1)}, bf16[1,256,128]{2,1,0:T(8,128)(2,1)S(1)}, u32[]{:S(2)}, u32[]{:S(2)}) collective-permute-start(bf16[1,256,128]{2,1,0:T(8,128)(2,1)S(1)} %get-tuple-element.107), channel_id=1, source_target_pairs={{1,0},{2,1},{3,2},{4,3},{5,4},{6,5},{7,6},{8,7},{9,8},{10,9},{11,1... | collective-permute-start | bytes 196616 | tf_op jit(solution)/shard_map/ppermute | solution.py:42
  169.1 3.0 %collective-permute-done.7 = bf16[1,256,128]{2,1,0:T(8,128)(2,1)S(1)} collective-permute-done((bf16[1,256,128]{2,1,0:T(8,128)(2,1)S(1)}, bf16[1,256,128]{2,1,0:T(8,128)(2,1)S(1)}, u32[]{:S(2)}, u32[]{:S(2)}) %collective-permute-start.7) | collective-permute-done | bytes 65568 | tf_op jit(solution)/shard_map/ppermute | solution.py:42
  172.4 1.5 fusion.73
  177.9 1.3 fusion.28
  (100 shorter events, 11.4 us)
Async XLA Ops:
  7.2 39.8 %copy-start = (bf16[1536,1024]{1,0:T(8,128)(2,1)S(1)}, bf16[1536,1024]{1,0:T(8,128)(2,1)}, u32[]{:S(2)}) copy-start(bf16[1536,1024]{1,0:T(8,128)(2,1)} %param.17) | copy-start | bytes 9437188
  7.2 9.5 %copy-start.9 = (f32[5,1536]{1,0:T(8,128)S(1)}, f32[5,1536]{1,0:T(8,128)}, u32[]{:S(2)}) copy-start(f32[5,1536]{1,0:T(8,128)} %param.15) | copy-start | bytes 92164
  7.2 71.9 %all-gather.2.cloned.1.call-start = ((), (), s32[]{:S(2)}) async-start(), calls=%async_computation | async-start | bytes 1671168 | tf_op jit(solution)/shard_map/all_gather | solution.py:128
  7.2 12.5 %copy-start.3 = (bf16[256,1536]{1,0:T(8,128)(2,1)S(1)}, bf16[256,1536]{1,0:T(8,128)(2,1)}, u32[]{:S(2)}) copy-start(bf16[256,1536]{1,0:T(8,128)(2,1)} %param.13) | copy-start | bytes 2359300
  8.8 13.4 %copy-start.10 = (bf16[1536,192]{0,1:T(8,128)(2,1)S(1)}, bf16[1536,192]{0,1:T(8,128)(2,1)}, u32[]{:S(2)}) copy-start(bf16[1536,192]{0,1:T(8,128)(2,1)} %param.19) | copy-start | bytes 1769476
  8.8 13.4 %copy-start.11 = (f32[1536]{0:T(1024)S(1)}, f32[1536]{0:T(1024)}, u32[]{:S(2)}) copy-start(f32[1536]{0:T(1024)} %param.16) | copy-start | bytes 18436
  10.3 6.6 %collective-permute-start = (bf16[2,1536]{1,0:T(2,128)(2,1)S(1)}, bf16[2,1536]{1,0:T(2,128)(2,1)S(1)}, u32[]{:S(2)}, u32[]{:S(2)}) collective-permute-start(bf16[2,1536]{1,0:T(2,128)(2,1)S(1)} %get-tuple-element.108), channel_id=1, source_target_pairs={{0,1},{1,2},{2,3},{3,4},{4,5},{5,6},{6,7},{7,8},{8,9},{9,10},{10,1... | collective-permute-start | bytes 18440 | tf_op jit(solution)/shard_map/ppermute | solution.py:40
  14.8 4.9 %collective-permute-start.1 = (bf16[2,1536]{1,0:T(2,128)(2,1)S(1)}, bf16[2,1536]{1,0:T(2,128)(2,1)S(1)}, u32[]{:S(2)}, u32[]{:S(2)}) collective-permute-start(bf16[2,1536]{1,0:T(2,128)(2,1)S(1)} %get-tuple-element.109), channel_id=1, source_target_pairs={{1,0},{2,1},{3,2},{4,3},{5,4},{6,5},{7,6},{8,7},{9,8},{10,9},{11,1... | collective-permute-start | bytes 18440 | tf_op jit(solution)/shard_map/ppermute | solution.py:42
  21.3 0.9 copy-start.4
  25.0 1.3 collective-permute-start.2
  26.4 5.9 %collective-permute-start.3 = (bf16[2,256,128]{2,1,0:T(8,128)(2,1)S(1)}, bf16[2,256,128]{2,1,0:T(8,128)(2,1)S(1)}, u32[]{:S(2)}, u32[]{:S(2)}) collective-permute-start(bf16[2,256,128]{2,1,0:T(8,128)(2,1)S(1)} %get-tuple-element.111), channel_id=1, source_target_pairs={{0,2},{1,3},{2,0},{3,1},{4,6},{5,7},{6,4},{7,5},{8,10},{9,11},{10,... | collective-permute-start | bytes 393224 | tf_op jit(solution)/shard_map/ppermute | solution.py:21
  32.4 9.8 %collective-permute-start.4 = (bf16[4,256,128]{2,1,0:T(8,128)(2,1)S(1)}, bf16[4,256,128]{2,1,0:T(8,128)(2,1)}, u32[]{:S(2)}, u32[]{:S(2)}) collective-permute-start(bf16[4,256,128]{2,1,0:T(8,128)(2,1)S(1)} %bitcast.132), channel_id=1, source_target_pairs={{0,4},{1,5},{2,6},{3,7},{4,0},{5,1},{6,2},{7,3},{8,12},{9,13},{10,... | collective-permute-start | bytes 786440 | tf_op jit(solution)/shard_map/ppermute | solution.py:21
  44.2 32.4 %collective-permute-start.5 = (bf16[8,256,128]{2,1,0:T(8,128)(2,1)}, bf16[8,256,128]{2,1,0:T(8,128)(2,1)}, u32[]{:S(2)}, u32[]{:S(2)}) collective-permute-start(bf16[8,256,128]{2,1,0:T(8,128)(2,1)} %bitcast.10), channel_id=1, source_target_pairs={{0,8},{1,9},{2,10},{3,11},{4,12},{5,13},{6,14},{7,15},{8,0},{9,1},... | collective-permute-start | bytes 1572872 | tf_op jit(solution)/shard_map/ppermute | solution.py:21
  83.7 1.4 copy-start.1
  87.3 1.1 copy-start.2
  90.3 1.4 copy-start.1
  93.9 1.1 copy-start.2
  96.9 1.4 copy-start.1
  100.5 1.1 copy-start.2
  103.5 1.4 copy-start.1
  107.2 1.1 copy-start.2
  110.2 1.4 copy-start.1
  113.8 1.1 copy-start.2
  116.8 1.4 copy-start.1
  120.4 1.1 copy-start.2
  123.4 1.4 copy-start.1
  127.0 1.1 copy-start.2
  130.0 1.4 copy-start.1
  133.6 1.1 copy-start.2
  134.8 1.6 copy-start.5
  136.4 4.9 %copy-start.7 = (bf16[1536,128]{1,0:T(8,128)(2,1)S(1)}, bf16[1536,128]{1,0:T(8,128)(2,1)}, u32[]{:S(2)}) copy-start(bf16[1536,128]{1,0:T(8,128)(2,1)} %param.22) | copy-start | bytes 1179652
  136.4 5.0 %copy-start.6 = (bf16[1536,128]{1,0:T(8,128)(2,1)S(1)}, bf16[1536,128]{1,0:T(8,128)(2,1)}, u32[]{:S(2)}) copy-start(bf16[1536,128]{1,0:T(8,128)(2,1)} %param.21) | copy-start | bytes 1179652
  164.5 4.5 %collective-permute-start.6 = (bf16[1,256,128]{2,1,0:T(8,128)(2,1)S(1)}, bf16[1,256,128]{2,1,0:T(8,128)(2,1)S(1)}, u32[]{:S(2)}, u32[]{:S(2)}) collective-permute-start(bf16[1,256,128]{2,1,0:T(8,128)(2,1)S(1)} %get-tuple-element.106), channel_id=1, source_target_pairs={{0,1},{1,2},{2,3},{3,4},{4,5},{5,6},{6,7},{7,8},{8,9},{9,10},{10,1... | collective-permute-start | bytes 196616 | tf_op jit(solution)/shard_map/ppermute | solution.py:40
  166.5 5.6 %collective-permute-start.7 = (bf16[1,256,128]{2,1,0:T(8,128)(2,1)S(1)}, bf16[1,256,128]{2,1,0:T(8,128)(2,1)S(1)}, u32[]{:S(2)}, u32[]{:S(2)}) collective-permute-start(bf16[1,256,128]{2,1,0:T(8,128)(2,1)S(1)} %get-tuple-element.107), channel_id=1, source_target_pairs={{1,0},{2,1},{3,2},{4,3},{5,4},{6,5},{7,6},{8,7},{9,8},{10,9},{11,1... | collective-permute-start | bytes 196616 | tf_op jit(solution)/shard_map/ppermute | solution.py:42
  172.4 1.5 copy-start.8
Sparse Core Ops, SparseCore 0:
  23.5 52.6 all-gather.1
